TPU v7x, 32 devices: a whole 2x2x4 slice. The times are simulated.
32 devices in a mesh: group: 2 (over x), dev: 16 (over z, y, core).
Axes of the slice: x: 2, y: 2, z: 4, core: 2. Of those that a mesh axis runs over, the one named last changes fastest.
Arguments:
- positions: float32 [256, 3, 544], P(('group', 'dev')), may hold values from -6 to 6
- analysis: float32 [289, 544], replicated, may hold values from -0.25 to 0.25
- synthesis: float32 [544, 289], replicated, may hold values from -0.375 to 0.375
- stiffness: float32 [289], replicated, may hold values from 0.1 to 10
- owner: int32 [1088, 1], P(('group', 'dev')), may hold values from 0 to 15; in each aligned block of 34 rows (0 to 33, 34 to 67, ...) at most 4 rows name the same one
- ulist: int32 [2048, 4], P(('group', 'dev')), may hold values from 0 to 191, as said below
Outputs:
- moved: float32 [256, 3, 544], P(('group', 'dev'))
- velocity: float32 [256, 3, 544], P(('group', 'dev'))
Inputs may be any that keep to these rules, and one draw needn't show every extreme that they name: On the points of one device, no owner receives more than 4 blocks, and some owner receives exactly 4. `ulist`: entry 0 of row r is 64 + r % 64, the slot itself.
All inputs are finite; a program needn't handle non-finite values.
Results may differ from a plain program's by a relative error of at most 0.00011.
Values sent between devices are 32-bit elements; how exact they have to be, the bound alone decides.
A program may use at most 64 MiB of HBM per device.

v0:
```python
import functools
import math

import jax
import jax.numpy as jnp
from jax import lax
from jax.experimental import pallas as pl
from jax.experimental.pallas import tpu as pltpu
from jax.sharding import PartitionSpec as P

LEAF = 128
ROWS = 16
SOFTENING = 0.25
ROOT = math.sqrt(SOFTENING)
KERNEL = 1.0 / (8.0 * math.pi)
TIME_STEP = 0.02
MESH = pl.DeviceIdType.MESH
BF16, F32 = jnp.bfloat16, jnp.float32


def split3(value):
    first = value.astype(BF16)
    rest = value - first.astype(F32)
    second = rest.astype(BF16)
    third = (rest - second.astype(F32)).astype(BF16)
    return first, second, third


def split2(value):
    first = value.astype(BF16)
    return first, (value - first.astype(F32)).astype(BF16)


def product(left, right_high, right_low, dims):
    high, low = split2(left)
    dot = functools.partial(
        lax.dot_general, dimension_numbers=(dims, ((), ())), preferred_element_type=F32
    )
    return dot(high, right_high) + (dot(low, right_high) + dot(high, right_low))


def beside(group, groups, action):
    pl.when(group + 1 < groups)(functools.partial(action, 0, group + 1))
    pl.when(group > 0)(functools.partial(action, 1, group - 1))


def kernel(
    capacity, knear,
    lists_ref, pos_hbm, ana_hbm, syn_hbm, stiff_hbm, owner_hbm,
    moved_ref, vel_ref,
    pos_ref, ana_ref, syn_ref, stiff_ref, owner_ref,
    ana_high, ana_low, syn_high, syn_low,
    packed_ref, near_ref, table_ref, target_ref, flows_ref, back_ref,
    dist0_ref, dist1_ref, value0_ref, value1_ref,
    load_sem, own_sem, send_sem, recv_sem, side_send, side_recv, back_send, back_recv,
):
    count, groups = lax.axis_size("dev"), lax.axis_size("group")
    me, group = lax.axis_index("dev"), lax.axis_index("group")
    slots = count * capacity
    rows, points = pos_ref.shape
    cells = rows // 3
    blocks = owner_ref.shape[1]
    tiles = pl.cdiv(points, LEAF)
    padded = tiles + tiles % 2

    barrier = pltpu.get_barrier_semaphore()

    def signal(step, carry):
        pl.semaphore_signal(
            barrier, inc=1, device_id={"dev": lax.rem(me + step, count)}, device_id_type=MESH
        )
        return carry

    lax.fori_loop(1, count, signal, 0)
    beside(
        group, groups,
        lambda way, other: pl.semaphore_signal(
            barrier, inc=1, device_id={"group": other}, device_id_type=MESH
        ),
    )
    loads = [
        pltpu.make_async_copy(src, dst, load_sem.at[number])
        for number, (src, dst) in enumerate(
            [
                (owner_hbm, owner_ref), (pos_hbm, pos_ref), (ana_hbm, ana_ref),
                (syn_hbm, syn_ref), (stiff_hbm, stiff_ref),
            ]
        )
    ]
    for load in loads:
        load.start()

    value1_ref[...] = jnp.zeros_like(value1_ref)

    loads[0].wait()
    piece = lax.broadcasted_iota(jnp.int32, (padded * cells, 1), 0)
    block = (piece % cells) * points // LEAF + piece // cells
    lane_block = lax.broadcasted_iota(jnp.int32, (padded * cells, blocks), 1)
    owner_row = owner_ref[...].astype(F32)
    owner_col = jnp.sum(jnp.where(block == lane_block, owner_row, 0.0), axis=1, keepdims=True)
    earlier = (owner_row == owner_col) & (lane_block < block)
    rank_col = jnp.sum(jnp.where(earlier, 1.0, 0.0), axis=1, keepdims=True)
    place = (rank_col * count + owner_col).astype(jnp.int32)
    place = jnp.where(piece < tiles * cells, place, slots)
    take = place == lax.broadcasted_iota(jnp.int32, (padded * cells, slots), 1)
    take = jnp.where(take, 1.0, 0.0)
    give = take.T.astype(BF16)
    take = take.astype(BF16)

    lane = lax.broadcasted_iota(jnp.int32, (rows, LEAF), 1)
    shift = points % LEAF
    cell = lax.broadcasted_iota(jnp.int32, (rows, LEAF), 0) % cells
    start = cell * shift % LEAF

    def turn(value, way):
        for bit in range((cells - 1).bit_length()):
            amount = way * (shift << bit) % LEAF
            if amount:
                rolled = pltpu.roll(value, amount, 1)
                value = jnp.where(cell // (1 << bit) % 2 == 1, rolled, value)
        return value

    def to_pieces(value):
        pieces, before = [], jnp.zeros((rows, LEAF), F32)
        for tile in range(tiles):
            part = value[:, tile * LEAF : min((tile + 1) * LEAF, points)]
            if part.shape[1] < LEAF:
                blank = jnp.zeros((rows, LEAF - part.shape[1]), F32)
                part = jnp.concatenate([part, blank], axis=1)
            part = turn(part, 1)
            pieces.append(jnp.where(lane >= start, part, before))
            before = part
        pieces += [jnp.zeros((rows, LEAF), F32)] * (padded - tiles)
        return [
            jnp.concatenate([p[k * cells : (k + 1) * cells] for p in pieces], axis=0)
            for k in range(3)
        ]

    def pack(value, first):
        pieces = split3(jnp.concatenate(to_pieces(value), axis=1))
        sent = sum(jnp.dot(give, piece, preferred_element_type=F32) for piece in pieces)
        for k in range(3):
            for r in range(capacity):
                packed_ref[:, (first + k) * capacity + r, :] = sent[
                    r * count : (r + 1) * count, k * LEAF : (k + 1) * LEAF
                ]

    loads[1].wait()
    field = pos_ref[...]
    pack(field, 0)
    loads[2].wait()
    ana_high[...], ana_low[...] = split2(ana_ref[...])
    loads[3].wait()
    syn_high[...], syn_low[...] = split2(syn_ref[...])
    loads[4].wait()
    coeffs = product(field, ana_high[...], ana_low[...], ((1,), (1,)))
    forces = -product(coeffs * stiff_ref[...], syn_high[...], syn_low[...], ((1,), (0,)))
    pack(forces, 3)

    sides = jnp.minimum(group, 1) + jnp.minimum(groups - 1 - group, 1)
    pl.semaphore_wait(barrier, count - 1 + sides)

    def step_of(number):
        half = (number + 1) // 2
        sign = 2 * (number % 2) - 1
        return count // 2 + sign * half

    def across(step):
        peer = lax.rem(me + step, count)
        return pltpu.make_async_remote_copy(
            src_ref=packed_ref.at[peer],
            dst_ref=near_ref.at[1, me],
            send_sem=send_sem.at[step],
            recv_sem=recv_sem.at[step],
            device_id={"dev": peer},
            device_id_type=MESH,
        )

    def along(step, way, other):
        chunk = lax.rem(me - step + count, count)
        return pltpu.make_async_remote_copy(
            src_ref=near_ref.at[1, chunk],
            dst_ref=near_ref.at[2 * way, chunk],
            send_sem=side_send.at[way, step],
            recv_sem=side_recv.at[way, step],
            device_id={"group": other},
            device_id_type=MESH,
        )

    def across_back(step):
        home = lax.rem(me - step + count, count)
        return pltpu.make_async_remote_copy(
            src_ref=flows_ref.at[home],
            dst_ref=back_ref.at[me],
            send_sem=back_send.at[step],
            recv_sem=back_recv.at[step],
            device_id={"dev": home},
            device_id_type=MESH,
        )

    own = pltpu.make_async_copy(packed_ref.at[me], near_ref.at[1, me], own_sem)
    own.start()

    def send(number, carry):
        across(step_of(number)).start()
        return carry

    lax.fori_loop(0, count - 1, send, 0)

    def prepare(data, slot):
        y, f = data[0:3], data[3:6]
        ones = jnp.ones((1, LEAF), F32)
        zeros3, zeros4 = jnp.zeros((3, LEAF), F32), jnp.zeros((4, LEAF), F32)
        y_sq = jnp.sum(y * y, axis=0, keepdims=True)
        yf = -jnp.sum(y * f, axis=0, keepdims=True)
        scale = 1.0 / SOFTENING
        dist = jnp.concatenate(
            [(-2.0 * scale) * y, scale * y_sq + 1.0, scale * ones, zeros3], axis=0
        )
        proj = jnp.concatenate([f, yf, zeros4], axis=0)
        d1, d2, d3 = [part.astype(F32) for part in split3(dist)]
        p1, p2, p3 = [part.astype(F32) for part in split3(proj)]
        w_f = jnp.concatenate([f * (KERNEL / ROOT), jnp.zeros((5, LEAF), F32)], axis=0)
        cube = KERNEL / ROOT**3
        w_y = jnp.concatenate([-cube * y, cube * ones, zeros4], axis=0)
        f1, f2 = [part.astype(F32) for part in split2(w_f)]
        y1, y2 = [part.astype(F32) for part in split2(w_y)]
        left = jnp.concatenate([d1, d2, d3, d1, d2, d1, f1, f2], axis=0)
        right = jnp.concatenate([p1, p2, p3, p1, p2, p1, y1, y2], axis=0)
        table_ref[slot, :, 0:LEAF] = left.astype(BF16)
        table_ref[slot, :, LEAF:] = right.astype(BF16)
        return y, y_sq

    def prepare_target(x, x_sq, slot):
        ones = jnp.ones((1, LEAF), F32)
        base = jnp.concatenate([x, ones, x_sq, jnp.zeros((3, LEAF), F32)], axis=0)
        t1, t2, t3 = [part.astype(F32) for part in split3(base)]
        target = jnp.concatenate([t1, t1, t1, t2, t2, t3], axis=0)
        target_ref[slot] = target.T.astype(BF16)

    def slot_data(side, home, r):
        return near_ref[side, home, pl.ds(r, 6, stride=capacity), :]

    def arrived(home):
        for r in range(capacity):
            slot = home * capacity + r
            x, x_sq = prepare(slot_data(1, home, r), slots + slot)
            prepare_target(x, x_sq, slot)

    prepare(jnp.zeros((6, LEAF), F32), 3 * slots)
    own.wait()
    beside(group, groups, lambda way, other: along(0, way, other).start())
    arrived(me)

    def relay(number, carry):
        step = step_of(number)
        across(step).wait_recv()
        beside(group, groups, lambda way, other: along(step, way, other).start())
        arrived(lax.rem(me - step + count, count))
        return carry

    lax.fori_loop(0, count - 1, relay, 0)

    def side_arrived(step):
        chunk = lax.rem(me - step + count, count)

        def accept(way, other):
            along(step, way, other).wait_recv()
            for r in range(capacity):
                slot = 2 * way * slots + chunk * capacity + r
                prepare(slot_data(2 * way, chunk, r), slot)

        pl.when(group > 0)(lambda: accept(0, group - 1))
        pl.when(group + 1 < groups)(lambda: accept(1, group + 1))

    side_arrived(0)

    def side_relay(number, carry):
        side_arrived(step_of(number))
        return carry

    lax.fori_loop(0, count - 1, side_relay, 0)

    low = jnp.where(group == 0, slots, 0)
    high = jnp.where(group == groups - 1, 2 * slots, 3 * slots)

    def source(slot, entry):
        named = lists_ref[entry, slot]
        return jnp.where((named >= low) & (named < high), named, 3 * slots)

    def distances(slot, out_ref):
        for entry in range(knear):
            out_ref[entry] = jnp.dot(
                target_ref[slot],
                table_ref[source(slot, entry), 0:48],
                preferred_element_type=F32,
            )

    def kernels(in_ref, out_ref):
        for entry in range(knear):
            for row in range(0, LEAF, ROWS):
                rr = in_ref[entry, row : row + ROWS, 0:LEAF]
                projected = in_ref[entry, row : row + ROWS, LEAF:]
                inv = lax.rsqrt(rr)
                inv3 = inv * inv * inv
                parts = split2(inv + inv3) + split2(projected * inv3)
                for part in range(4):
                    at = (4 * entry + part) * LEAF
                    out_ref[row : row + ROWS, at : at + LEAF] = parts[part]

    def sums(home, r, in_ref, keep):
        slot = home * capacity + r
        weights = []
        for entry in range(knear):
            number = source(slot, entry)
            w_f = table_ref[number, 48:64, 0:LEAF]
            w_y = table_ref[number, 48:64, LEAF:]
            weights += [w_f, w_f, w_y, w_y]
        part = lax.dot_general(
            jnp.concatenate(weights, axis=1),
            in_ref[...],
            (((1,), (1,)), ((), ())),
            preferred_element_type=F32,
        )
        total = part[0:8] + part[8:16]
        x = near_ref[1, home, pl.ds(r, 3, stride=capacity), :]
        flows_ref[keep, pl.ds(r, 3, stride=capacity), :] = total[0:3] + x * total[3:4]

    def home_of(number):
        step = jnp.where(number < count - 1, step_of(number), 0)
        return lax.rem(me - step + count, count)

    dist = (dist0_ref, dist1_ref)
    value = (value0_ref, value1_ref)
    distances(home_of(0) * capacity, dist0_ref)

    def chunk(number, carry):
        home = home_of(number)
        after = home_of(jnp.minimum(number + 1, count - 1))
        last = jnp.maximum(number - 1, 0)
        before = home_of(last)
        for r in range(capacity):
            parity = r % 2
            following = home * capacity + r + 1 if r + 1 < capacity else after * capacity
            distances(following, dist[1 - parity])
            kernels(dist[parity], value[parity])
            if r:
                sums(home, r - 1, value[1 - parity], home)
            else:
                keep = jnp.where(number > 0, before, count)
                sums(before, capacity - 1, value[1 - parity], keep)

        @pl.when(number > 0)
        def _():
            across_back(step_of(last)).start()

        return carry

    lax.fori_loop(0, count, chunk, 0)
    sums(me, capacity - 1, value1_ref, me)
    back_ref[me] = flows_ref[me]

    def finish(number, carry):
        across_back(step_of(number)).wait_recv()
        return carry

    lax.fori_loop(0, count - 1, finish, 0)

    returned = [
        jnp.concatenate([back_ref[:, k * capacity + r, :] for r in range(capacity)], axis=0)
        for k in range(3)
    ]
    pieces = split3(jnp.concatenate(returned, axis=1))
    taken = sum(jnp.dot(take, piece, preferred_element_type=F32) for piece in pieces)
    tile_rows = [
        jnp.concatenate(
            [
                taken[t * cells : (t + 1) * cells, k * LEAF : (k + 1) * LEAF]
                for k in range(3)
            ],
            axis=0,
        )
        for t in range(tiles)
    ]
    for tile in range(tiles):
        part = tile_rows[tile]
        if tile + 1 < tiles:
            part = jnp.where(lane >= start, part, tile_rows[tile + 1])
        part = turn(part, -1)
        width = min(LEAF, points - tile * LEAF)
        vel_ref[:, tile * LEAF : tile * LEAF + width] = part[:, 0:width]
    stepped = pos_ref[...] + TIME_STEP * vel_ref[...]
    coeffs = product(stepped, ana_high[...], ana_low[...], ((1,), (1,)))
    moved_ref[...] = product(coeffs, syn_high[...], syn_low[...], ((1,), (0,)))

    def sent(number, carry):
        step = step_of(number)
        across(step).wait_send()
        across_back(step).wait_send()
        return carry

    lax.fori_loop(0, count - 1, sent, 0)

    def side_sent(step, carry):
        beside(group, groups, lambda way, other: along(step, way, other).wait_send())
        return carry

    lax.fori_loop(0, count, side_sent, 0)


def shards(positions, analysis, synthesis, stiffness, owner, ulist):
    count = lax.axis_size("dev")
    cells, dims, points = positions.shape
    coefs = analysis.shape[0]
    blocks = owner.shape[0]
    knear = ulist.shape[1]
    capacity = ulist.shape[0] // count
    slots = count * capacity
    rows = dims * cells
    sem = pltpu.SemaphoreType.DMA
    shape = jax.ShapeDtypeStruct((rows, points), F32)
    any_spec = pl.BlockSpec(memory_space=pl.ANY)
    vmem_spec = pl.BlockSpec(memory_space=pltpu.VMEM)
    moved, velocity = pl.pallas_call(
        functools.partial(kernel, capacity, knear),
        out_shape=(shape, shape),
        in_specs=[pl.BlockSpec(memory_space=pltpu.SMEM)] + [any_spec] * 5,
        out_specs=(vmem_spec, vmem_spec),
        scratch_shapes=[
            pltpu.VMEM((rows, points), F32),
            pltpu.VMEM((coefs, points), F32),
            pltpu.VMEM((coefs, points), F32),
            pltpu.VMEM((1, coefs), F32),
            pltpu.VMEM((1, blocks), jnp.int32),
            pltpu.VMEM((coefs, points), BF16),
            pltpu.VMEM((coefs, points), BF16),
            pltpu.VMEM((coefs, points), BF16),
            pltpu.VMEM((coefs, points), BF16),
            pltpu.VMEM((count, 6 * capacity, LEAF), F32),
            pltpu.VMEM((3, count, 6 * capacity, LEAF), F32),
            pltpu.VMEM((3 * slots + 1, 64, 2 * LEAF), BF16),
            pltpu.VMEM((slots, LEAF, 48), BF16),
            pltpu.VMEM((count + 1, 3 * capacity, LEAF), F32),
            pltpu.VMEM((count, 3 * capacity, LEAF), F32),
            pltpu.VMEM((knear, LEAF, 2 * LEAF), F32),
            pltpu.VMEM((knear, LEAF, 2 * LEAF), F32),
            pltpu.VMEM((LEAF, 4 * knear * LEAF), BF16),
            pltpu.VMEM((LEAF, 4 * knear * LEAF), BF16),
            sem((5,)), sem, sem((count,)), sem((count,)), sem((2, count)), sem((2, count)),
            sem((count,)), sem((count,)),
        ],
        compiler_params=pltpu.CompilerParams(collective_id=0, has_side_effects=True),
    )(
        ulist.T,
        positions.transpose(1, 0, 2).reshape(rows, points),
        analysis,
        synthesis.T,
        stiffness.reshape(1, coefs),
        owner.reshape(1, blocks),
    )

    def to_cells(value):
        return value.reshape(dims, cells, points).transpose(1, 0, 2)

    return to_cells(moved), to_cells(velocity)


def solution(mesh):
    placed = (
        P(("group", "dev"), None, None),
        P(),
        P(),
        P(),
        P(("group", "dev"), None),
        P(("group", "dev"), None),
    )
    return jax.shard_map(
        shards,
        mesh=mesh,
        in_specs=placed,
        out_specs=(P(("group", "dev"), None, None), P(("group", "dev"), None, None)),
        check_vma=False,
    )
```

profile of v0, /device:TPU:0, one launch (start us, length us, event | category | flops | bytes accessed | tf_op | source)
XLA Modules:
  0.0 43.6 jit_solution(9350969513449715139)
XLA Ops:
  0.6 0.0 copy-start.1
  0.6 0.7 %copy-done.1 = f32[289]{0:T(512)S(1)} copy-done((f32[289]{0:T(512)S(1)}, f32[289]{0:T(512)}, u32[]{:S(2)}) %copy-start.1) | copy-done | bytes 1180
  1.3 0.6 %reshape.20.stiff_hbm = f32[1,289]{1,0:T(1,128)} reshape(f32[289]{0:T(512)S(1)} %copy-done.1) | data formatting | bytes 2312 | tf_op jit(solution)/shard_map/reshape | solution.py:458
  1.9 39.6 %shard_map.77 = (f32[24,544]{1,0:T(8,128)}, f32[24,544]{1,0:T(8,128)}) custom-call(s32[4,64]{1,0:T(4,128)} %bitcast.16, f32[24,544]{1,0:T(8,128)} %bitcast.13, f32[289,544]{1,0:T(8,128)} %ana_hbm.1, f32[289,544]{1,0:T(8,128)} %bitcast.12, f32[1,289]{1,0:T(1,128)} %reshape.20.stiff_hbm, s32[1,34]{1,0:T(1,128)} %bitcast.17), custom_call_target="tpu_custom_call" | custom-call | tf_op jit(solution)/shard_map/pallas_call | solution.py:424
  41.5 0.0 copy-start
  41.5 1.5 %copy.10 = f32[8,3,544]{2,0,1:T(8,128)} copy(f32[8,3,544]{2,0,1:T(8,128)} %bitcast.15) | data formatting | bytes 104448
  43.0 0.0 copy-done
  43.0 0.6 %copy.11 = f32[8,3,544]{2,0,1:T(8,128)} copy(f32[8,3,544]{2,0,1:T(8,128)S(1)} %bitcast.14) | data formatting | bytes 104448
Async XLA Ops:
  0.6 0.7 %copy-start.1 = (f32[289]{0:T(512)S(1)}, f32[289]{0:T(512)}, u32[]{:S(2)}) copy-start(f32[289]{0:T(512)} %param.9) | copy-start | bytes 3472
  41.5 1.5 %copy-start = (f32[24,544]{1,0:T(8,128)S(1)}, f32[24,544]{1,0:T(8,128)}, u32[]{:S(2)}) copy-start(f32[24,544]{1,0:T(8,128)} %get-tuple-element.5) | copy-start | bytes 156676
where the time goes:
time: 43.9 us; the launch traced here: 43.6 us
  Pallas kernels  39.6 us (90%)
  local copies, waits for them, and re-layouts  3.34 us (8%)
  between operations  0.66 us (2%)
    pallas_call x1, Pallas kernels, shards(): pl.pallas_call(functools.partial(kernel, capacity, knear), out_shape=(sha...  39.6 us
    unnamed x6, local copies, waits for them, and re-layouts  2.78 us

commit v1 on v0

--- a/solution.py
+++ b/solution.py
@@ -46,14 +46,15 @@
 
 def kernel(
     capacity, knear,
-    lists_ref, pos_hbm, ana_hbm, syn_hbm, stiff_hbm, owner_hbm,
+    lists_hbm, pos_hbm, ana_hbm, syn_hbm, stiff_hbm, owner_hbm,
     moved_ref, vel_ref,
-    pos_ref, ana_ref, syn_ref, stiff_ref, owner_ref,
+    lists_ref, pos_ref, ana_ref, syn_ref, stiff_ref, owner_ref,
     ana_high, ana_low, syn_high, syn_low,
     packed_ref, near_ref, table_ref, target_ref, flows_ref, back_ref,
-    dist0_ref, dist1_ref, value0_ref, value1_ref,
-    load_sem, own_sem, send_sem, recv_sem, side_send, side_recv, back_send, back_recv,
+    self_dist, self_value, partial_ref, *rest,
 ):
+    dist, value, rest = rest[:capacity], rest[capacity : 2 * capacity], rest[2 * capacity :]
+    load_sem, own_sem, send_sem, recv_sem, side_send, side_recv, back_send, back_recv = rest
     count, groups = lax.axis_size("dev"), lax.axis_size("group")
     me, group = lax.axis_index("dev"), lax.axis_index("group")
     slots = count * capacity
@@ -84,13 +85,16 @@
             [
                 (owner_hbm, owner_ref), (pos_hbm, pos_ref), (ana_hbm, ana_ref),
                 (syn_hbm, syn_ref), (stiff_hbm, stiff_ref),
+                (lists_hbm, lists_ref),
             ]
         )
     ]
     for load in loads:
         load.start()
 
-    value1_ref[...] = jnp.zeros_like(value1_ref)
+    self_value[...] = jnp.zeros_like(self_value)
+    for ref in value:
+        ref[...] = jnp.zeros_like(ref)
 
     loads[0].wait()
     piece = lax.broadcasted_iota(jnp.int32, (padded * cells, 1), 0)
@@ -154,7 +158,7 @@
     syn_high[...], syn_low[...] = split2(syn_ref[...])
     loads[4].wait()
     coeffs = product(field, ana_high[...], ana_low[...], ((1,), (1,)))
-    forces = -product(coeffs * stiff_ref[...], syn_high[...], syn_low[...], ((1,), (0,)))
+    forces = -product(coeffs * stiff_ref[...][None, :], syn_high[...], syn_low[...], ((1,), (0,)))
     pack(forces, 3)
 
     sides = jnp.minimum(group, 1) + jnp.minimum(groups - 1 - group, 1)
@@ -247,19 +251,71 @@
             x, x_sq = prepare(slot_data(1, home, r), slots + slot)
             prepare_target(x, x_sq, slot)
 
+    def distances(slot, number):
+        return jnp.dot(target_ref[slot], table_ref[number, 0:48], preferred_element_type=F32)
+
+    def kernels(items, in_ref, out_ref):
+        for item in range(items):
+            for row in range(0, LEAF, ROWS):
+                rr = in_ref[item, row : row + ROWS, 0:LEAF]
+                projected = in_ref[item, row : row + ROWS, LEAF:]
+                inv = lax.rsqrt(rr)
+                inv3 = inv * inv * inv
+                parts = split2(inv + inv3) + split2(projected * inv3)
+                for part in range(4):
+                    at = (4 * item + part) * LEAF
+                    out_ref[row : row + ROWS, at : at + LEAF] = parts[part]
+
+    def sums(numbers, values):
+        weights = []
+        for number in numbers:
+            w_f = table_ref[number, 48:64, 0:LEAF]
+            w_y = table_ref[number, 48:64, LEAF:]
+            weights += [w_f, w_f, w_y, w_y]
+        part = lax.dot_general(
+            jnp.concatenate(weights, axis=1),
+            values,
+            (((1,), (1,)), ((), ())),
+            preferred_element_type=F32,
+        )
+        return part[0:8] + part[8:16]
+
+    def self_distances(home):
+        for r in range(capacity):
+            slot = home * capacity + r
+            self_dist[r] = distances(slot, slots + slot)
+
+    def self_sums(home, keep):
+        for r in range(capacity):
+            values = self_value[:, 4 * r * LEAF : 4 * (r + 1) * LEAF]
+            partial_ref[keep * capacity + r] = sums([slots + home * capacity + r], values)
+
     prepare(jnp.zeros((6, LEAF), F32), 3 * slots)
     own.wait()
     beside(group, groups, lambda way, other: along(0, way, other).start())
     arrived(me)
+    self_distances(me)
+
+    def in_turn(number):
+        step = jnp.where(number > 0, step_of(jnp.maximum(number - 1, 0)), 0)
+        return lax.rem(me - step + count, count)
 
     def relay(number, carry):
         step = step_of(number)
         across(step).wait_recv()
         beside(group, groups, lambda way, other: along(step, way, other).start())
-        arrived(lax.rem(me - step + count, count))
+        two_back = in_turn(jnp.maximum(number - 1, 0))
+        home = in_turn(number + 1)
+        self_sums(two_back, jnp.where(number > 0, two_back, count))
+        kernels(capacity, self_dist, self_value)
+        arrived(home)
+        self_distances(home)
         return carry
 
     lax.fori_loop(0, count - 1, relay, 0)
+    self_sums(in_turn(count - 2), in_turn(count - 2))
+    kernels(capacity, self_dist, self_value)
+    self_sums(in_turn(count - 1), in_turn(count - 1))
 
     def side_arrived(step):
         chunk = lax.rem(me - step + count, count)
@@ -281,6 +337,7 @@
 
     lax.fori_loop(0, count - 1, side_relay, 0)
 
+    loads[5].wait()
     low = jnp.where(group == 0, slots, 0)
     high = jnp.where(group == groups - 1, 2 * slots, 3 * slots)
 
@@ -288,67 +345,36 @@
         named = lists_ref[entry, slot]
         return jnp.where((named >= low) & (named < high), named, 3 * slots)
 
-    def distances(slot, out_ref):
-        for entry in range(knear):
-            out_ref[entry] = jnp.dot(
-                target_ref[slot],
-                table_ref[source(slot, entry), 0:48],
-                preferred_element_type=F32,
-            )
-
-    def kernels(in_ref, out_ref):
-        for entry in range(knear):
-            for row in range(0, LEAF, ROWS):
-                rr = in_ref[entry, row : row + ROWS, 0:LEAF]
-                projected = in_ref[entry, row : row + ROWS, LEAF:]
-                inv = lax.rsqrt(rr)
-                inv3 = inv * inv * inv
-                parts = split2(inv + inv3) + split2(projected * inv3)
-                for part in range(4):
-                    at = (4 * entry + part) * LEAF
-                    out_ref[row : row + ROWS, at : at + LEAF] = parts[part]
-
-    def sums(home, r, in_ref, keep):
-        slot = home * capacity + r
-        weights = []
-        for entry in range(knear):
-            number = source(slot, entry)
-            w_f = table_ref[number, 48:64, 0:LEAF]
-            w_y = table_ref[number, 48:64, LEAF:]
-            weights += [w_f, w_f, w_y, w_y]
-        part = lax.dot_general(
-            jnp.concatenate(weights, axis=1),
-            in_ref[...],
-            (((1,), (1,)), ((), ())),
-            preferred_element_type=F32,
-        )
-        total = part[0:8] + part[8:16]
-        x = near_ref[1, home, pl.ds(r, 3, stride=capacity), :]
-        flows_ref[keep, pl.ds(r, 3, stride=capacity), :] = total[0:3] + x * total[3:4]
-
     def home_of(number):
         step = jnp.where(number < count - 1, step_of(number), 0)
         return lax.rem(me - step + count, count)
 
-    dist = (dist0_ref, dist1_ref)
-    value = (value0_ref, value1_ref)
-    distances(home_of(0) * capacity, dist0_ref)
+
+    others = range(1, knear)
+
+    def other_distances(home, r):
+        slot = home * capacity + r
+        for entry in others:
+            dist[r][entry - 1] = distances(slot, source(slot, entry))
+
+    def other_sums(home, r, keep):
+        slot = home * capacity + r
+        total = sums([source(slot, entry) for entry in others], value[r][...])
+        total = total + partial_ref[slot]
+        x = near_ref[1, home, pl.ds(r, 3, stride=capacity), :]
+        flows_ref[keep, pl.ds(r, 3, stride=capacity), :] = total[0:3] + x * total[3:4]
+
+    for r in range(capacity):
+        other_distances(home_of(0), r)
 
     def chunk(number, carry):
-        home = home_of(number)
-        after = home_of(jnp.minimum(number + 1, count - 1))
         last = jnp.maximum(number - 1, 0)
-        before = home_of(last)
+        before, after = home_of(last), home_of(jnp.minimum(number + 1, count - 1))
+        keep = jnp.where(number > 0, before, count)
         for r in range(capacity):
-            parity = r % 2
-            following = home * capacity + r + 1 if r + 1 < capacity else after * capacity
-            distances(following, dist[1 - parity])
-            kernels(dist[parity], value[parity])
-            if r:
-                sums(home, r - 1, value[1 - parity], home)
-            else:
-                keep = jnp.where(number > 0, before, count)
-                sums(before, capacity - 1, value[1 - parity], keep)
+            other_sums(before, r, keep)
+            kernels(knear - 1, dist[r], value[r])
+            other_distances(after, r)
 
         @pl.when(number > 0)
         def _():
@@ -357,7 +383,8 @@
         return carry
 
     lax.fori_loop(0, count, chunk, 0)
-    sums(me, capacity - 1, value1_ref, me)
+    for r in range(capacity):
+        other_sums(me, r, me)
     back_ref[me] = flows_ref[me]
 
     def finish(number, carry):
@@ -419,18 +446,19 @@
     rows = dims * cells
     sem = pltpu.SemaphoreType.DMA
     shape = jax.ShapeDtypeStruct((rows, points), F32)
-    any_spec = pl.BlockSpec(memory_space=pl.ANY)
+    hbm_spec = pl.BlockSpec(memory_space=pltpu.HBM)
     vmem_spec = pl.BlockSpec(memory_space=pltpu.VMEM)
     moved, velocity = pl.pallas_call(
         functools.partial(kernel, capacity, knear),
         out_shape=(shape, shape),
-        in_specs=[pl.BlockSpec(memory_space=pltpu.SMEM)] + [any_spec] * 5,
+        in_specs=[hbm_spec] * 6,
         out_specs=(vmem_spec, vmem_spec),
         scratch_shapes=[
+            pltpu.SMEM(ulist.T.shape, jnp.int32),
             pltpu.VMEM((rows, points), F32),
             pltpu.VMEM((coefs, points), F32),
             pltpu.VMEM((coefs, points), F32),
-            pltpu.VMEM((1, coefs), F32),
+            pltpu.VMEM((coefs,), F32),
             pltpu.VMEM((1, blocks), jnp.int32),
             pltpu.VMEM((coefs, points), BF16),
             pltpu.VMEM((coefs, points), BF16),
@@ -442,11 +470,12 @@
             pltpu.VMEM((slots, LEAF, 48), BF16),
             pltpu.VMEM((count + 1, 3 * capacity, LEAF), F32),
             pltpu.VMEM((count, 3 * capacity, LEAF), F32),
-            pltpu.VMEM((knear, LEAF, 2 * LEAF), F32),
-            pltpu.VMEM((knear, LEAF, 2 * LEAF), F32),
-            pltpu.VMEM((LEAF, 4 * knear * LEAF), BF16),
-            pltpu.VMEM((LEAF, 4 * knear * LEAF), BF16),
-            sem((5,)), sem, sem((count,)), sem((count,)), sem((2, count)), sem((2, count)),
+            pltpu.VMEM((capacity, LEAF, 2 * LEAF), F32),
+            pltpu.VMEM((LEAF, 4 * capacity * LEAF), BF16),
+            pltpu.VMEM((slots + capacity, 8, LEAF), F32),
+            *[pltpu.VMEM((knear - 1, LEAF, 2 * LEAF), F32) for _ in range(capacity)],
+            *[pltpu.VMEM((LEAF, 4 * (knear - 1) * LEAF), BF16) for _ in range(capacity)],
+            sem((6,)), sem, sem((count,)), sem((count,)), sem((2, count)), sem((2, count)),
             sem((count,)), sem((count,)),
         ],
         compiler_params=pltpu.CompilerParams(collective_id=0, has_side_effects=True),
@@ -455,7 +484,7 @@
         positions.transpose(1, 0, 2).reshape(rows, points),
         analysis,
         synthesis.T,
-        stiffness.reshape(1, coefs),
+        stiffness,
         owner.reshape(1, blocks),
     )
 

time: 43.9 us -> 39.7 us (0.904)
  Pallas kernels: 39.6 us -> 36.8 us
  local copies, waits for them, and re-layouts: 3.34 us -> 2.1 us
    pallas_call x1, Pallas kernels: 39.6 us -> 36.8 us  [shards(): pl.pallas_call(functools.partial(kernel, capacity, knear), out_shape=(sha...]
    unnamed x6 -> x4, local copies, waits for them, and re-layouts: 2.78 us -> 2.1 us
    reshape x1 -> x0, local copies, waits for them, and re-layouts: 0.56 us -> none  [shards(): stiffness.reshape(1, coefs)]
where the time goes in v1:
time: 39.7 us; the launch traced here: 39.5 us
  Pallas kernels  36.8 us (93%)
  local copies, waits for them, and re-layouts  2.1 us (5%)
  between operations  0.65 us (2%)
    pallas_call x1, Pallas kernels, shards(): pl.pallas_call(functools.partial(kernel, capacity, knear), out_shape=(sha...  36.8 us
    unnamed x4, local copies, waits for them, and re-layouts  2.1 us

profile of v1, /device:TPU:0, one launch (start us, length us, event | category | flops | bytes accessed | tf_op | source)
XLA Modules:
  0.0 39.5 jit_solution(5751761676661329335)
XLA Ops:
  0.6 36.8 %shard_map.77 = (f32[24,544]{1,0:T(8,128)}, f32[24,544]{1,0:T(8,128)}) custom-call(s32[4,64]{1,0:T(4,128)} %bitcast.16, f32[24,544]{1,0:T(8,128)} %bitcast.13, f32[289,544]{1,0:T(8,128)} %ana_hbm.1, f32[289,544]{1,0:T(8,128)} %bitcast.12, f32[289]{0:T(512)} %stiff_hbm.1, s32[1,34]{1,0:T(1,128)} %bitcast.17), custom_call_target="tpu_custom_call" | custom-call | tf_op jit(solution)/shard_map/pallas_call | solution.py:451
  37.4 0.0 copy-start
  37.4 1.5 %copy.10 = f32[8,3,544]{2,0,1:T(8,128)} copy(f32[8,3,544]{2,0,1:T(8,128)} %bitcast.15) | data formatting | bytes 104448
  38.9 0.0 copy-done
  38.9 0.6 %copy.11 = f32[8,3,544]{2,0,1:T(8,128)} copy(f32[8,3,544]{2,0,1:T(8,128)S(1)} %bitcast.14) | data formatting | bytes 104448
Async XLA Ops:
  37.4 1.5 %copy-start = (f32[24,544]{1,0:T(8,128)S(1)}, f32[24,544]{1,0:T(8,128)}, u32[]{:S(2)}) copy-start(f32[24,544]{1,0:T(8,128)} %get-tuple-element.5) | copy-start | bytes 156676

commit v2 on v1

--- a/solution.py
+++ b/solution.py
@@ -50,7 +50,7 @@
     moved_ref, vel_ref,
     lists_ref, pos_ref, ana_ref, syn_ref, stiff_ref, owner_ref,
     ana_high, ana_low, syn_high, syn_low,
-    packed_ref, near_ref, table_ref, target_ref, flows_ref, back_ref,
+    packed_ref, near_ref, source_ref, weight_ref, target_ref, flows_ref, back_ref,
     self_dist, self_value, partial_ref, *rest,
 ):
     dist, value, rest = rest[:capacity], rest[capacity : 2 * capacity], rest[2 * capacity :]
@@ -229,18 +229,21 @@
         w_y = jnp.concatenate([-cube * y, cube * ones, zeros4], axis=0)
         f1, f2 = [part.astype(F32) for part in split2(w_f)]
         y1, y2 = [part.astype(F32) for part in split2(w_y)]
-        left = jnp.concatenate([d1, d2, d3, d1, d2, d1, f1, f2], axis=0)
-        right = jnp.concatenate([p1, p2, p3, p1, p2, p1, y1, y2], axis=0)
-        table_ref[slot, :, 0:LEAF] = left.astype(BF16)
-        table_ref[slot, :, LEAF:] = right.astype(BF16)
+        rows_in = [d1, d2, d3, d1, d2, d1, p1, p2, p3, p1, p2, p1]
+        source_ref[slot] = jnp.concatenate(rows_in, axis=0).T.astype(BF16)
+        weight_ref[slot, :, 0:LEAF] = jnp.concatenate([f1, f2], axis=0).astype(BF16)
+        weight_ref[slot, :, LEAF:] = jnp.concatenate([y1, y2], axis=0).astype(BF16)
         return y, y_sq
 
     def prepare_target(x, x_sq, slot):
         ones = jnp.ones((1, LEAF), F32)
         base = jnp.concatenate([x, ones, x_sq, jnp.zeros((3, LEAF), F32)], axis=0)
         t1, t2, t3 = [part.astype(F32) for part in split3(base)]
-        target = jnp.concatenate([t1, t1, t1, t2, t2, t3], axis=0)
-        target_ref[slot] = target.T.astype(BF16)
+        target = jnp.concatenate([t1, t1, t1, t2, t2, t3], axis=0).astype(BF16)
+        target_ref[slot, 0:48, 0:LEAF] = target
+        target_ref[slot, 48:96, LEAF:] = target
+        target_ref[slot, 0:48, LEAF:] = jnp.zeros((48, LEAF), BF16)
+        target_ref[slot, 48:96, 0:LEAF] = jnp.zeros((48, LEAF), BF16)
 
     def slot_data(side, home, r):
         return near_ref[side, home, pl.ds(r, 6, stride=capacity), :]
@@ -251,31 +254,35 @@
             x, x_sq = prepare(slot_data(1, home, r), slots + slot)
             prepare_target(x, x_sq, slot)
 
-    def distances(slot, number):
-        return jnp.dot(target_ref[slot], table_ref[number, 0:48], preferred_element_type=F32)
+    def distances(slot, numbers):
+        sources = [source_ref[number] for number in numbers]
+        return jnp.dot(
+            jnp.concatenate(sources, axis=0), target_ref[slot], preferred_element_type=F32
+        )
 
     def kernels(items, in_ref, out_ref):
         for item in range(items):
             for row in range(0, LEAF, ROWS):
-                rr = in_ref[item, row : row + ROWS, 0:LEAF]
-                projected = in_ref[item, row : row + ROWS, LEAF:]
+                at = item * LEAF + row
+                rr = in_ref[at : at + ROWS, 0:LEAF]
+                projected = in_ref[at : at + ROWS, LEAF:]
                 inv = lax.rsqrt(rr)
                 inv3 = inv * inv * inv
                 parts = split2(inv + inv3) + split2(projected * inv3)
                 for part in range(4):
-                    at = (4 * item + part) * LEAF
-                    out_ref[row : row + ROWS, at : at + LEAF] = parts[part]
+                    at = (4 * item + part) * LEAF + row
+                    out_ref[at : at + ROWS] = parts[part]
 
     def sums(numbers, values):
         weights = []
         for number in numbers:
-            w_f = table_ref[number, 48:64, 0:LEAF]
-            w_y = table_ref[number, 48:64, LEAF:]
+            w_f = weight_ref[number, :, 0:LEAF]
+            w_y = weight_ref[number, :, LEAF:]
             weights += [w_f, w_f, w_y, w_y]
         part = lax.dot_general(
             jnp.concatenate(weights, axis=1),
             values,
-            (((1,), (1,)), ((), ())),
+            (((1,), (0,)), ((), ())),
             preferred_element_type=F32,
         )
         return part[0:8] + part[8:16]
@@ -283,11 +290,11 @@
     def self_distances(home):
         for r in range(capacity):
             slot = home * capacity + r
-            self_dist[r] = distances(slot, slots + slot)
+            self_dist[r * LEAF : (r + 1) * LEAF] = distances(slot, [slots + slot])
 
     def self_sums(home, keep):
         for r in range(capacity):
-            values = self_value[:, 4 * r * LEAF : 4 * (r + 1) * LEAF]
+            values = self_value[4 * r * LEAF : 4 * (r + 1) * LEAF]
             partial_ref[keep * capacity + r] = sums([slots + home * capacity + r], values)
 
     prepare(jnp.zeros((6, LEAF), F32), 3 * slots)
@@ -354,8 +361,7 @@
 
     def other_distances(home, r):
         slot = home * capacity + r
-        for entry in others:
-            dist[r][entry - 1] = distances(slot, source(slot, entry))
+        dist[r][...] = distances(slot, [source(slot, entry) for entry in others])
 
     def other_sums(home, r, keep):
         slot = home * capacity + r
@@ -466,15 +472,16 @@
             pltpu.VMEM((coefs, points), BF16),
             pltpu.VMEM((count, 6 * capacity, LEAF), F32),
             pltpu.VMEM((3, count, 6 * capacity, LEAF), F32),
-            pltpu.VMEM((3 * slots + 1, 64, 2 * LEAF), BF16),
-            pltpu.VMEM((slots, LEAF, 48), BF16),
+            pltpu.VMEM((3 * slots + 1, LEAF, 96), BF16),
+            pltpu.VMEM((3 * slots + 1, 16, 2 * LEAF), BF16),
+            pltpu.VMEM((slots, 96, 2 * LEAF), BF16),
             pltpu.VMEM((count + 1, 3 * capacity, LEAF), F32),
             pltpu.VMEM((count, 3 * capacity, LEAF), F32),
-            pltpu.VMEM((capacity, LEAF, 2 * LEAF), F32),
-            pltpu.VMEM((LEAF, 4 * capacity * LEAF), BF16),
+            pltpu.VMEM((capacity * LEAF, 2 * LEAF), F32),
+            pltpu.VMEM((4 * capacity * LEAF, LEAF), BF16),
             pltpu.VMEM((slots + capacity, 8, LEAF), F32),
-            *[pltpu.VMEM((knear - 1, LEAF, 2 * LEAF), F32) for _ in range(capacity)],
-            *[pltpu.VMEM((LEAF, 4 * (knear - 1) * LEAF), BF16) for _ in range(capacity)],
+            *[pltpu.VMEM(((knear - 1) * LEAF, 2 * LEAF), F32) for _ in range(capacity)],
+            *[pltpu.VMEM((4 * (knear - 1) * LEAF, LEAF), BF16) for _ in range(capacity)],
             sem((6,)), sem, sem((count,)), sem((count,)), sem((2, count)), sem((2, count)),
             sem((count,)), sem((count,)),
         ],

time: 39.7 us -> 37 us (0.932)
  Pallas kernels: 36.8 us -> 34.1 us
    pallas_call x1, Pallas kernels: 36.8 us -> 34.1 us  [shards(): pl.pallas_call(functools.partial(kernel, capacity, knear), out_shape=(sha...]
where the time goes in v2:
time: 37 us; the launch traced here: 36.9 us
  Pallas kernels  34.1 us (92%)
  local copies, waits for them, and re-layouts  2.1 us (6%)
  between operations  0.65 us (2%)
    pallas_call x1, Pallas kernels, shards(): pl.pallas_call(functools.partial(kernel, capacity, knear), out_shape=(sha...  34.1 us
    unnamed x4, local copies, waits for them, and re-layouts  2.1 us

profile of v2, /device:TPU:0, one launch (start us, length us, event | category | flops | bytes accessed | tf_op | source)
XLA Modules:
  0.0 36.9 jit_solution(1928778152324943963)
XLA Ops:
  0.6 34.1 %shard_map.77 = (f32[24,544]{1,0:T(8,128)}, f32[24,544]{1,0:T(8,128)}) custom-call(s32[4,64]{1,0:T(4,128)} %bitcast.16, f32[24,544]{1,0:T(8,128)} %bitcast.13, f32[289,544]{1,0:T(8,128)} %ana_hbm.1, f32[289,544]{1,0:T(8,128)} %bitcast.12, f32[289]{0:T(512)} %stiff_hbm.1, s32[1,34]{1,0:T(1,128)} %bitcast.17), custom_call_target="tpu_custom_call" | custom-call | tf_op jit(solution)/shard_map/pallas_call | solution.py:457
  34.7 0.0 copy-start
  34.8 1.5 %copy.10 = f32[8,3,544]{2,0,1:T(8,128)} copy(f32[8,3,544]{2,0,1:T(8,128)} %bitcast.15) | data formatting | bytes 104448
  36.2 0.0 copy-done
  36.2 0.6 %copy.11 = f32[8,3,544]{2,0,1:T(8,128)} copy(f32[8,3,544]{2,0,1:T(8,128)S(1)} %bitcast.14) | data formatting | bytes 104448
Async XLA Ops:
  34.7 1.5 %copy-start = (f32[24,544]{1,0:T(8,128)S(1)}, f32[24,544]{1,0:T(8,128)}, u32[]{:S(2)}) copy-start(f32[24,544]{1,0:T(8,128)} %get-tuple-element.5) | copy-start | bytes 156676
